TPU v7x, 32 devices: a whole 2x2x4 slice. The times are simulated.
32 devices in a mesh: shots: 2 (over y), freq: 4 (over x, core), tile: 4 (over z).
Axes of the slice: x: 2, y: 2, z: 4, core: 2. Of those that a mesh axis runs over, the one named last changes fastest.
Arguments:
- velocity: float32 [4, 96, 1024], P(None, 'tile', 'freq'), may hold values from 1.5 to 4.5
- src_cell: int32 [8192], P('shots'), parts along dimension 0, may hold values from 0 to 98303
- src_wave: float32 [2, 4, 8192], P(None, 'freq', 'shots'), parts along dimension 2, may hold values from -24 to 24
- rec_cell: int32 [32768], P('shots'), parts along dimension 0, may hold values from 0 to 98303
- rec_data: float32 [2, 4, 32768], P(None, 'freq', 'shots'), parts along dimension 2, may hold values from -24 to 24
Outputs:
- final_fields: float32 [4, 4, 2, 96, 1024], P('shots', 'freq', None, 'tile'), parts along dimension 0
- migrated_image: float32 [8, 96, 1024], P('shots', 'tile', 'freq'), parts along dimension 0
There are 2 independent parts, one for each index of `shots`. A program takes and returns all parts, laid end to end along the dimension named above; an argument that names none is the same for every part. Nothing has to cross between parts.
Inputs may be any that keep to these rules, and one draw needn't show every extreme that they name: `src_cell`: each entry is a surface cell numbered row * 1024 + column; cells may repeat. `rec_cell`: each entry is a surface cell numbered row * 1024 + column; cells may repeat.
All inputs are finite; a program needn't handle non-finite values.
Results may differ from a plain program's by a relative error of at most 0.00002.
Values sent between devices are 32-bit elements; how exact they have to be, the bound alone decides.
No kernel may reach another device: no remote copies, remote signals or barrier semaphores. Data moves between devices by JAX's collectives and lax.ppermute only.
A program may use at most 128 MiB of HBM per device.

v0:
```python
import functools

import jax
import jax.numpy as jnp
from jax import lax
from jax.experimental import pallas as pl
from jax.experimental.pallas import tpu as pltpu
from jax.sharding import PartitionSpec as P

PASSES = 5
LANES = 128
SUB = 8
CHUNK = 1024
UNROLL = 4
BLOCK = 256

term_weights = (0.3, 0.25, -0.15, 0.12, -0.1, 0.08)
phase_unit = 0.25
slowest = 1.5


def round_up(value, unit):
    return -(-value // unit) * unit


def inject_kernel(rows, halo, row_count, cell_ref, wave_ref, out_ref):
    chunk = min(CHUNK, cell_ref.shape[0] * LANES)
    chunks = cell_ref.shape[0] * LANES // chunk
    blocks = out_ref.shape[1] // 2
    pair = 2 * LANES
    cols = blocks * pair
    high_count = blocks * rows
    tall = 2 * SUB
    first = lax.axis_index("tile") * row_count - halo
    size = min(BLOCK, max(high_count, pair))
    ids = lax.broadcasted_iota(jnp.int32, (size, LANES), 0).astype(jnp.float32).astype(jnp.bfloat16)

    def spread(values, line, count):
        one = jnp.broadcast_to(values[line : line + 1], (tall, LANES)).astype(jnp.bfloat16)
        return jnp.concatenate([one] * (count // tall), axis=0)

    def one_hot(index, line, count):
        return jnp.maximum(1.0 - jnp.abs(ids[:count] - spread(index, line, count)), 0.0)

    def add(index):
        lines = chunk // LANES
        lefts, rights = [], []
        for group in range(0, lines, SUB):
            height = min(SUB, lines)
            at = pl.ds(pl.multiple_of(index * lines + group, height), height)
            cell = cell_ref[at, :]
            row = cell // cols - first
            col = cell % cols
            high = jnp.where((row >= 0) & (row < rows), col // pair * rows + row, -1)
            low = ((col % 2) * LANES + col % pair // 2).astype(jnp.float32)
            pieces = []
            for part in range(2):
                value = wave_ref[part, at, :]
                top = value.astype(jnp.bfloat16).astype(jnp.float32)
                pieces += [top, value - top]
            for line in range(height):
                rights.append(one_hot(low, line, pair))
                variants = [[] for _ in pieces]
                for base in range(0, high_count, size):
                    count = min(size, high_count - base)
                    match = one_hot((high - base).astype(jnp.float32), line, count)
                    for variant, piece in zip(variants, pieces):
                        variant.append(match * spread(piece, line, count))
                lefts.append(jnp.concatenate(sum(variants, []), axis=0))
        total = lax.dot_general(
            jnp.concatenate(lefts, axis=1),
            jnp.concatenate(rights, axis=1),
            (((1,), (1,)), ((), ())),
            preferred_element_type=jnp.float32,
        )
        for part in range(2):
            at = 2 * part * high_count
            both = total[at : at + high_count] + total[at + high_count : at + 2 * high_count]
            for odd in range(2):
                out_at = slice(odd * blocks, (odd + 1) * blocks)
                out_ref[part, out_at] = out_ref[part, out_at] + both[:, odd * LANES : (odd + 1) * LANES].reshape(
                    blocks, rows, LANES
                )

    out_ref[...] = jnp.zeros_like(out_ref)
    unroll = next(u for u in (UNROLL, 2, 1) if chunks % u == 0)

    def some_chunks(index, carry):
        for one in range(unroll):
            add(index * unroll + one)
        return carry

    lax.fori_loop(0, chunks // unroll, some_chunks, 0)


def inject(cells, waves, rows, halo, row_count, cols):
    points = cells.shape[0]
    whole = pl.BlockSpec(memory_space=pltpu.VMEM)
    return pl.pallas_call(
        functools.partial(inject_kernel, rows, halo, row_count),
        out_shape=jax.ShapeDtypeStruct((2, cols // LANES, rows, LANES), jnp.float32),
        in_specs=[whole, whole],
        out_specs=whole,
        cost_estimate=pl.CostEstimate(
            flops=8 * rows * cols * points, bytes_accessed=12 * points, transcendentals=0
        ),
        name="inject",
    )(cells.reshape(points // LANES, LANES), waves.reshape(2, points // LANES, LANES))


def sine(angle, square, terms):
    total = None
    for k in range(terms - 1, 0, -1):
        coef = 1.0
        for m in range(2, 2 * k + 2):
            coef /= m
        coef = coef if k % 2 == 0 else -coef
        total = coef if total is None else total * square + coef
    return angle * (total * square + 1.0)


def cosine(square, terms):
    total = None
    for k in range(terms - 1, 0, -1):
        coef = 1.0
        for m in range(2, 2 * k + 1):
            coef /= m
        coef = coef if k % 2 == 0 else -coef
        total = coef if total is None else total * square + coef
    return total * square + 1.0


def terms_for(largest, offset):
    count, size = 1, largest * largest / ((1 + offset) * (2 + offset))
    while size > 3e-8 or count < 2:
        count += 1
        size *= largest * largest / ((2 * count - 1 + offset) * (2 * count + offset))
    return count


def times(a, b):
    return a[0] * b[0] - a[1] * b[1], a[0] * b[1] + a[1] * b[0]


def squared(a):
    twice = a[1] + a[1]
    return 1.0 - twice * a[1], twice * a[0]


def coefficients(speed, number, limit):
    slow = (0.2 * phase_unit) * number / jnp.maximum(speed, 1.0)
    square = slow * slow
    sines, cosines = terms_for(0.2 * limit, 1), terms_for(0.2 * limit, 0)
    a20 = (cosine(square, cosines), sine(slow, square, sines))
    small, square = slow * 0.75, square * 0.5625
    a15 = (cosine(square, cosines), sine(small, square, sines))
    a30 = squared(a15)
    a45 = times(a30, a15)
    a60 = squared(a30)
    a80 = times(a60, a20)
    a100 = times(a80, a20)
    angles = (a100, a80, a60, a45, a30, a20)
    return [(weight * a[0], weight * a[1]) for weight, a in zip(term_weights, angles)]


def depth_kernel(sizes, *refs):
    row_count, steps, halo, vel_halo = sizes
    freqs = lax.axis_size("freq")
    tiles = lax.axis_size("tile")
    pieces, (before_ref, after_ref, src_ref, rec_ref) = refs[:freqs], refs[freqs : freqs + 4]
    fields_ref, *image_refs = refs[freqs + 4 : 2 * freqs + 5]
    terms, sums, speed, flat, sem = refs[2 * freqs + 5 :]
    me = lax.axis_index("freq")
    tile = lax.axis_index("tile")
    number = (me + 1).astype(jnp.float32)
    limit = freqs * phase_unit / slowest
    rows = row_count + 2 * halo
    parts = src_ref.shape[1]
    blocks = parts // 2
    width = pieces[0].shape[-1]
    per_owner = width // LANES

    pending = []

    def copy(src, dst):
        pending.append(pltpu.make_async_copy(src, dst, sem.at[copy.started]))
        pending[-1].start()
        copy.started += 1

    def finish():
        while pending:
            pending.pop(0).wait()

    copy.started = 0
    for field, ref in enumerate((src_ref, rec_ref)):
        for part in range(2):
            copy(ref.at[part], terms.at[0, 2 * field + part, :, :rows, :])
    arrived = pending[:]
    for back, piece in enumerate(pieces):
        owner = lax.rem(me + freqs - back, freqs)
        for part in range(per_owner):
            lanes = slice(part * LANES, (part + 1) * LANES)
            for ref, low, size in (
                (piece, vel_halo, row_count),
                (before_ref.at[back], 0, vel_halo),
                (after_ref.at[back], vel_halo + row_count, vel_halo),
            ):
                copy(ref.at[:, :, lanes], speed.at[:, owner * per_owner + part, low : low + size, :])

    shape = (SUB, LANES)
    lane = lax.broadcasted_iota(jnp.int32, shape, 1)
    sub = lax.broadcasted_iota(jnp.int32, shape, 0)
    first_lane, last_lane = lane == 0, lane == LANES - 1
    zero = jnp.zeros(shape, jnp.float32)
    edges = (
        (halo - 1, jnp.where(tile == 0, 0.0, 1.0)),
        (halo + row_count, jnp.where(tile == tiles - 1, 0.0, 1.0)),
    )

    def strided(low, count, index=0):
        return pl.ds(low + index, SUB, stride=count)

    def take(value, index):
        return jnp.take_along_axis(value, index, axis=1, mode="promise_in_bounds")

    def split(low, high):
        index = (2 * lane) % LANES
        return [
            jnp.where(lane < LANES // 2, take(low, index + odd), take(high, index + odd)) for odd in range(2)
        ]

    def join(even, odd):
        index = lane // 2
        return [
            jnp.where(lane % 2 == 1, take(odd, index + at), take(even, index + at)) for at in (0, LANES // 2)
        ]

    def share(low, high):
        count = -(-(high - low) // SUB)
        return count + (count % SUB == 0)

    for one in arrived:
        one.wait()
        pending.remove(one)

    def one_pass(order, low, high):
        count = share(low, high)
        keeps = {}
        for row, keep in edges:
            at, index = divmod(row - low, count)
            if 0 <= at < SUB:
                keeps.setdefault(index, []).append(jnp.where(sub == at, keep, 1.0))

        def plane_body(plane, carry):
            def load(part, index):
                return terms[order - 1, plane, part, strided(low, count, index), :]

            here = [load(part, 0) for part in range(parts)]
            pair = [load(part, -1) + here[part] for part in range(parts)]
            for index in range(count):
                below = [load(part, index + 1) for part in range(parts)]
                next_pair = [here[part] + below[part] for part in range(parts)]
                stacked = [pair[part] + next_pair[part] for part in range(parts)]
                moved = [pltpu.roll(v, LANES - 1 if part < blocks else 1, 1) for part, v in enumerate(stacked)]
                for part in range(parts):
                    blk = part % blocks
                    even, odd = stacked[blk], stacked[blocks + blk]
                    if part < blocks:
                        other = moved[part + blocks - 1] if blk > 0 else zero
                        side = jnp.where(first_lane, other, moved[part + blocks])
                        total = (even + odd) + even + side
                    else:
                        other = moved[blk + 1] if blk + 1 < blocks else zero
                        side = jnp.where(last_lane, other, moved[blk])
                        total = (even + odd) + odd + side
                    at = strided(low, count, index)
                    if order == 1:
                        total = 0.125 * total
                    else:
                        total = 0.25 * total - sums[plane, part, at, :]
                    new = total - here[part]
                    for keep in keeps.get(index, []):
                        new = new * keep
                        total = total * keep
                    if order < PASSES:
                        sums[plane, part, at, :] = total
                    terms[order, plane, part, at, :] = new
                here, pair = below, next_pair
            return carry

        lax.fori_loop(0, 4, plane_body, 0)

    def put(slot, blk, at, pair):
        for half, value in enumerate(join(*pair)):
            flat[slot, 2 * blk + half, at, :] = value

    for step in range(steps):
        for order in range(1, PASSES + 1):
            one_pass(order, PASSES * step + order, rows - PASSES * step - order)
        low, high = PASSES * (step + 1), rows - PASSES * (step + 1)
        count = share(low, high)
        last = step == steps - 1
        if step == 0:
            finish()

        def blend(index, carry):
            at = strided(low, count, index)
            vel_at = strided(low - halo + vel_halo, count, index)
            for blk in range(blocks):
                done = []
                speeds = split(*[speed[step, 2 * blk + half, vel_at, :] for half in range(2)])
                for odd in range(2):
                    part = odd * blocks + blk
                    coefs = coefficients(speeds[odd], number, limit)
                    results = []
                    for field in range(2):
                        real, imag = [], []
                        for order, (cr, ci) in enumerate(coefs):
                            tr = terms[order, 2 * field, part, at, :]
                            ti = terms[order, 2 * field + 1, part, at, :]
                            if field == 0:
                                real += [cr * tr - ci * ti]
                                imag += [cr * ti + ci * tr]
                            else:
                                real += [cr * tr + ci * ti]
                                imag += [cr * ti - ci * tr]
                        results += [sum(real[1:], real[0]), sum(imag[1:], imag[0])]
                    if last:
                        results.append(results[0] * results[2] + results[1] * results[3])
                    else:
                        for plane in range(4):
                            terms[0, plane, part, at, :] = results[plane]
                    done.append(results)
                if last:
                    out_at = strided(0, count, index)
                    for slot, pair in zip((0, 1, 2, 3, 4 + step), zip(*done)):
                        put(slot, blk, out_at, pair)
            return carry

        lax.fori_loop(0, count, blend, 0)
        if not last:
            image_count = row_count // SUB

            def correlate(index, carry):
                for blk in range(blocks):
                    pair = []
                    for odd in range(2):
                        field = [
                            terms[0, plane, odd * blocks + blk, strided(halo, image_count, index), :]
                            for plane in range(4)
                        ]
                        pair.append(field[0] * field[2] + field[1] * field[3])
                    put(4 + step, blk, strided(0, image_count, index), pair)
                return carry

            lax.fori_loop(0, image_count, correlate, 0)

        for ahead, ref in enumerate(image_refs):
            owner = lax.rem(me + ahead, freqs)
            for part in range(per_owner):
                lanes = slice(part * LANES, (part + 1) * LANES)
                copy(flat.at[4 + step, owner * per_owner + part], ref.at[step, :, lanes])
    for plane in range(4):
        for part in range(parts):
            lanes = slice(part * LANES, (part + 1) * LANES)
            copy(flat.at[plane, part], fields_ref.at[plane // 2, 0, plane % 2, :, lanes])
    finish()


def depth_steps(pieces, before, after, src, rec, sizes):
    row_count, steps, halo, vel_halo = sizes
    width = pieces[0].shape[-1]
    owners = len(pieces)
    rows = row_count + 2 * halo
    parts = owners * width // LANES
    tall = row_count + 2 * vel_halo
    there = pl.BlockSpec(memory_space=pltpu.HBM)
    return pl.pallas_call(
        functools.partial(depth_kernel, sizes),
        out_shape=(
            jax.ShapeDtypeStruct((2, 1, 2, row_count, owners * width), jnp.float32),
            *[jax.ShapeDtypeStruct((steps, row_count, width), jnp.float32)] * owners,
        ),
        in_specs=[there] * (owners + 4),
        out_specs=(there,) * (owners + 1),
        scratch_shapes=[
            pltpu.VMEM((PASSES + 1, 4, parts, rows + 2 * SUB, LANES), jnp.float32),
            pltpu.VMEM((4, parts, rows + 2 * SUB, LANES), jnp.float32),
            pltpu.VMEM((steps, parts, tall + 2 * SUB, LANES), jnp.float32),
            pltpu.VMEM((4 + steps, parts, row_count, LANES), jnp.float32),
            pltpu.SemaphoreType.DMA((4 + 3 * parts + (4 + steps) * parts,)),
        ],
        cost_estimate=pl.CostEstimate(
            flops=steps * 300 * rows * owners * width, bytes_accessed=64 * rows * owners * width, transcendentals=0
        ),
        name="depth",
    )(*pieces, before, after, src, rec)


def shifts(axis):
    count = lax.axis_size(axis)
    return [[(i, (i + k) % count) for i in range(count)] for k in range(1, count)]


def body(velocity, src_cell, src_wave, rec_cell, rec_data):
    steps, row_count, width = velocity.shape
    freqs, tiles = lax.axis_size("freq"), lax.axis_size("tile")
    assert width % LANES == 0 and width * freqs % (2 * LANES) == 0 and row_count % SUB == 0
    me = lax.axis_index("freq")
    halo = PASSES * steps
    vel_halo = round_up(PASSES * (steps - 1), SUB)
    rows = row_count + 2 * halo
    sizes = (row_count, steps, halo, vel_halo)

    cols = width * freqs
    others = [lax.ppermute(velocity, "freq", pairs) for pairs in shifts("freq")]
    src = inject(src_cell, src_wave, rows, halo, row_count, cols)
    others, src = lax.optimization_barrier((others, src))
    pieces = [velocity] + others
    up = [(i, i + 1) for i in range(tiles - 1)]
    down = [(j, i) for i, j in up]
    lowest = jnp.stack([p[:, row_count - vel_halo :] for p in pieces])
    highest = jnp.stack([p[:, :vel_halo] for p in pieces])
    lowest, highest, rec_cell = lax.optimization_barrier((lowest, highest, rec_cell))
    before = lax.ppermute(lowest, "tile", up)
    after = lax.ppermute(highest, "tile", down)
    rec = inject(rec_cell, rec_data, rows, halo, row_count, cols)
    fields, total, *images = depth_steps(pieces, before, after, src, rec, sizes)
    for image, pairs in zip(images, shifts("freq")):
        total = total + lax.ppermute(image, "freq", pairs)
    return fields, total


def solution(mesh):
    placed = (
        P(None, "tile", "freq"),
        P("shots"),
        P(None, "freq", "shots"),
        P("shots"),
        P(None, "freq", "shots"),
    )
    return jax.shard_map(
        body,
        mesh=mesh,
        in_specs=placed,
        out_specs=(P("shots", "freq", None, "tile", None), P("shots", "tile", "freq")),
        check_vma=False,
    )
```

profile of v0, /device:TPU:0, one launch (start us, length us, event | category | flops | bytes accessed | tf_op | source)
XLA Modules:
  0.0 56.1 jit_solution(14594039838594935789)
XLA Ops:
  0.6 2.5 %collective-permute-start.2 = (f32[4,24,256]{2,1,0:T(8,128)}, f32[4,24,256]{2,1,0:T(8,128)S(1)}, u32[]{:S(2)}, u32[]{:S(2)}) collective-permute-start(f32[4,24,256]{2,1,0:T(8,128)} %refs_0_.1), channel_id=1, source_target_pairs={{0,12},{4,0},{8,4},{12,8},{1,13},{5,1},{9,5},{13,9},{2,14},{6,2},{... | collective-permute-start | bytes 294920 | tf_op jit(solution)/shard_map/ppermute | solution.py:416
  3.1 0.6 %collective-permute-start.1 = (f32[4,24,256]{2,1,0:T(8,128)}, f32[4,24,256]{2,1,0:T(8,128)S(1)}, u32[]{:S(2)}, u32[]{:S(2)}) collective-permute-start(f32[4,24,256]{2,1,0:T(8,128)} %refs_0_.1), channel_id=1, source_target_pairs={{0,8},{4,12},{8,0},{12,4},{1,9},{5,13},{9,1},{13,5},{2,10},{6,14},... | collective-permute-start | bytes 294920 | tf_op jit(solution)/shard_map/ppermute | solution.py:416
  3.7 0.1 collective-permute-start
  3.9 0.9 %slice_bitcast_fusion.3 = (f32[1,4,16,256]{3,2,1,0:T(8,128)S(1)}, f32[1,4,16,256]{3,2,1,0:T(8,128)S(1)}) fusion(f32[4,24,256]{2,1,0:T(8,128)} %refs_0_.1), kind=kLoop, calls=%fused_computation.6 | loop fusion | bytes 262144 | tf_op jit(solution)/shard_map/stack | solution.py:423
  4.8 4.0 %inject.2.refs_6_ = f32[2,8,64,128]{3,2,1,0:T(8,128)} custom-call(s32[32,128]{1,0:T(8,128)} %bitcast.23, f32[2,32,128]{2,1,0:T(8,128)} %bitcast.22), custom_call_target="tpu_custom_call" | custom-call | flops 2147483648 | bytes 49152 | tf_op jit(solution)/shard_map/inject/pallas_call | solution.py:99
  8.8 0.0 collective-permute-done.2.refs_3_
  8.8 0.0 copy-start.1
  8.8 0.7 %collective-permute-done.1.refs_2_ = f32[4,24,256]{2,1,0:T(8,128)S(1)} collective-permute-done((f32[4,24,256]{2,1,0:T(8,128)}, f32[4,24,256]{2,1,0:T(8,128)S(1)}, u32[]{:S(2)}, u32[]{:S(2)}) %collective-permute-start.1) | collective-permute-done | bytes 98336 | tf_op jit(solution)/shard_map/ppermute | solution.py:416
  9.4 0.0 copy-start.2
  9.4 0.0 collective-permute-done.refs_1_
  9.4 0.0 copy-start
  9.5 0.0 copy-done.1
  9.5 0.6 %copy-done = f32[4,24,256]{2,1,0:T(8,128)} copy-done((f32[4,24,256]{2,1,0:T(8,128)}, f32[4,24,256]{2,1,0:T(8,128)S(1)}, u32[]{:S(2)}) %copy-start) | copy-done | bytes 98328
  10.1 0.0 copy-done.2
  10.2 3.6 %collective-permute-start.3 = (f32[4,4,16,256]{3,2,1,0:T(8,128)S(1)}, f32[4,4,16,256]{3,2,1,0:T(8,128)S(1)}, u32[]{:S(2)}, u32[]{:S(2)}) collective-permute-start(f32[4,4,16,256]{3,2,1,0:T(8,128)S(1)} %pad_maximum_fusion), channel_id=1, source_target_pairs={{0,1},{1,2},{2,3},{4,5},{5,6},{6,7},{8,9},{9,10},{10,11},{12,13},{... | collective-permute-start | bytes 786440 | tf_op jit(solution)/shard_map/ppermute | solution.py:425
  13.9 1.3 %collective-permute-start.4 = (f32[4,4,16,256]{3,2,1,0:T(8,128)S(1)}, f32[4,4,16,256]{3,2,1,0:T(8,128)S(1)}, u32[]{:S(2)}, u32[]{:S(2)}) collective-permute-start(f32[4,4,16,256]{3,2,1,0:T(8,128)S(1)} %pad_maximum_fusion.1), channel_id=1, source_target_pairs={{1,0},{2,1},{3,2},{5,4},{6,5},{7,6},{9,8},{10,9},{11,10},{13,12},{... | collective-permute-start | bytes 786440 | tf_op jit(solution)/shard_map/ppermute | solution.py:426
  15.2 11.4 %inject.3.refs_7_ = f32[2,8,64,128]{3,2,1,0:T(8,128)} custom-call(s32[128,128]{1,0:T(8,128)} %bitcast.21, f32[2,128,128]{2,1,0:T(8,128)} %bitcast.20), custom_call_target="tpu_custom_call" | custom-call | flops 8589934592 | bytes 196608 | tf_op jit(solution)/shard_map/inject/pallas_call | solution.py:99
  26.5 0.0 collective-permute-done.3.refs_4_
  26.5 0.0 copy-start.3
  26.5 0.0 collective-permute-done.4.refs_5_
  26.5 0.7 %copy-done.3 = f32[4,4,16,256]{3,2,1,0:T(8,128)} copy-done((f32[4,4,16,256]{3,2,1,0:T(8,128)}, f32[4,4,16,256]{3,2,1,0:T(8,128)S(1)}, u32[]{:S(2)}) %copy-start.3) | copy-done | bytes 262168
  27.3 0.0 copy-start.4
  27.3 0.7 %copy-done.4 = f32[4,4,16,256]{3,2,1,0:T(8,128)} copy-done((f32[4,4,16,256]{3,2,1,0:T(8,128)}, f32[4,4,16,256]{3,2,1,0:T(8,128)S(1)}, u32[]{:S(2)}) %copy-start.4) | copy-done | bytes 262168
  28.0 20.0 %depth.1 = (f32[2,1,2,24,1024]{4,3,2,1,0:T(8,128)}, f32[4,24,256]{2,1,0:T(8,128)}, f32[4,24,256]{2,1,0:T(8,128)}, f32[4,24,256]{2,1,0:T(8,128)}, f32[4,24,256]{2,1,0:T(8,128)}) custom-call(f32[4,24,256]{2,1,0:T(8,128)} %refs_0_.1, f32[4,24,256]{2,1,0:T(8,128)} %copy-done, f32[4,24,256]{2,1,0:T(8,128)} %copy-done.2, f32[4,24,256]{2,1,0:T(8,128)} %copy-done.1, ...), custom_call_target="tpu_custom_call" | custom-call | flops 78643200 | bytes 4194304 | tf_op jit(solution)/shard_map/depth/pallas_call | solution.py:378
  48.0 0.3 collective-permute-start.5
  48.3 1.3 %collective-permute-start.6 = (f32[4,24,256]{2,1,0:T(8,128)}, f32[4,24,256]{2,1,0:T(8,128)S(1)}, u32[]{:S(2)}, u32[]{:S(2)}) collective-permute-start(f32[4,24,256]{2,1,0:T(8,128)} %get-tuple-element.24), channel_id=1, source_target_pairs={{0,8},{4,12},{8,0},{12,4},{1,9},{5,13},{9,1},{13,5},{2,10},{6,14},... | collective-permute-start | bytes 294920 | tf_op jit(solution)/shard_map/ppermute | solution.py:430
  49.6 1.4 %collective-permute-start.7 = (f32[4,24,256]{2,1,0:T(8,128)}, f32[4,24,256]{2,1,0:T(8,128)S(1)}, u32[]{:S(2)}, u32[]{:S(2)}) collective-permute-start(f32[4,24,256]{2,1,0:T(8,128)} %get-tuple-element.25), channel_id=1, source_target_pairs={{0,12},{4,0},{8,4},{12,8},{1,13},{5,1},{9,5},{13,9},{2,14},{6,2},{... | collective-permute-start | bytes 294920 | tf_op jit(solution)/shard_map/ppermute | solution.py:430
  51.0 1.5 %collective-permute-done.5 = f32[4,24,256]{2,1,0:T(8,128)S(1)} collective-permute-done((f32[4,24,256]{2,1,0:T(8,128)}, f32[4,24,256]{2,1,0:T(8,128)S(1)}, u32[]{:S(2)}, u32[]{:S(2)}) %collective-permute-start.5) | collective-permute-done | bytes 98336 | tf_op jit(solution)/shard_map/ppermute | solution.py:430
  52.5 1.7 %collective-permute-done.6 = f32[4,24,256]{2,1,0:T(8,128)S(1)} collective-permute-done((f32[4,24,256]{2,1,0:T(8,128)}, f32[4,24,256]{2,1,0:T(8,128)S(1)}, u32[]{:S(2)}, u32[]{:S(2)}) %collective-permute-start.6) | collective-permute-done | bytes 98336 | tf_op jit(solution)/shard_map/ppermute | solution.py:430
  54.2 0.3 collective-permute-done.7
  54.5 1.6 %add_add_fusion = f32[4,24,256]{2,1,0:T(8,128)} fusion(f32[4,24,256]{2,1,0:T(8,128)S(1)} %collective-permute-done.7, f32[4,24,256]{2,1,0:T(8,128)S(1)} %collective-permute-done.6, f32[4,24,256]{2,1,0:T(8,128)} %get-tuple-element.22, f32[4,24,256]{2,1,0:T(8,128)S(1)} %collective-permute-done.5), kind=kLoop, calls=%fused_computation.2 | loop fusion | flops 73728 | bytes 491520 | tf_op jit(solution)/shard_map/add | solution.py:430
  (4 shorter events, 0.1 us)
Async XLA Ops:
  0.6 8.1 %collective-permute-start.2 = (f32[4,24,256]{2,1,0:T(8,128)}, f32[4,24,256]{2,1,0:T(8,128)S(1)}, u32[]{:S(2)}, u32[]{:S(2)}) collective-permute-start(f32[4,24,256]{2,1,0:T(8,128)} %refs_0_.1), channel_id=1, source_target_pairs={{0,12},{4,0},{8,4},{12,8},{1,13},{5,1},{9,5},{13,9},{2,14},{6,2},{... | collective-permute-start | bytes 294920 | tf_op jit(solution)/shard_map/ppermute | solution.py:416
  3.1 6.3 %collective-permute-start.1 = (f32[4,24,256]{2,1,0:T(8,128)}, f32[4,24,256]{2,1,0:T(8,128)S(1)}, u32[]{:S(2)}, u32[]{:S(2)}) collective-permute-start(f32[4,24,256]{2,1,0:T(8,128)} %refs_0_.1), channel_id=1, source_target_pairs={{0,8},{4,12},{8,0},{12,4},{1,9},{5,13},{9,1},{13,5},{2,10},{6,14},... | collective-permute-start | bytes 294920 | tf_op jit(solution)/shard_map/ppermute | solution.py:416
  3.7 5.7 %collective-permute-start = (f32[4,24,256]{2,1,0:T(8,128)}, f32[4,24,256]{2,1,0:T(8,128)S(1)}, u32[]{:S(2)}, u32[]{:S(2)}) collective-permute-start(f32[4,24,256]{2,1,0:T(8,128)} %refs_0_.1), channel_id=1, source_target_pairs={{0,4},{4,8},{8,12},{12,0},{1,5},{5,9},{9,13},{13,1},{2,6},{6,10},{... | collective-permute-start | bytes 294920 | tf_op jit(solution)/shard_map/ppermute | solution.py:416
  8.8 0.7 %copy-start.1 = (f32[4,24,256]{2,1,0:T(8,128)}, f32[4,24,256]{2,1,0:T(8,128)S(1)}, u32[]{:S(2)}) copy-start(f32[4,24,256]{2,1,0:T(8,128)S(1)} %collective-permute-done.2.refs_3_) | copy-start | bytes 294916
  9.4 0.7 %copy-start.2 = (f32[4,24,256]{2,1,0:T(8,128)}, f32[4,24,256]{2,1,0:T(8,128)S(1)}, u32[]{:S(2)}) copy-start(f32[4,24,256]{2,1,0:T(8,128)S(1)} %collective-permute-done.1.refs_2_) | copy-start | bytes 294916
  9.4 0.7 %copy-start = (f32[4,24,256]{2,1,0:T(8,128)}, f32[4,24,256]{2,1,0:T(8,128)S(1)}, u32[]{:S(2)}) copy-start(f32[4,24,256]{2,1,0:T(8,128)S(1)} %collective-permute-done.refs_1_) | copy-start | bytes 294916
  10.2 16.3 %collective-permute-start.3 = (f32[4,4,16,256]{3,2,1,0:T(8,128)S(1)}, f32[4,4,16,256]{3,2,1,0:T(8,128)S(1)}, u32[]{:S(2)}, u32[]{:S(2)}) collective-permute-start(f32[4,4,16,256]{3,2,1,0:T(8,128)S(1)} %pad_maximum_fusion), channel_id=1, source_target_pairs={{0,1},{1,2},{2,3},{4,5},{5,6},{6,7},{8,9},{9,10},{10,11},{12,13},{... | collective-permute-start | bytes 786440 | tf_op jit(solution)/shard_map/ppermute | solution.py:425
  13.9 12.7 %collective-permute-start.4 = (f32[4,4,16,256]{3,2,1,0:T(8,128)S(1)}, f32[4,4,16,256]{3,2,1,0:T(8,128)S(1)}, u32[]{:S(2)}, u32[]{:S(2)}) collective-permute-start(f32[4,4,16,256]{3,2,1,0:T(8,128)S(1)} %pad_maximum_fusion.1), channel_id=1, source_target_pairs={{1,0},{2,1},{3,2},{5,4},{6,5},{7,6},{9,8},{10,9},{11,10},{13,12},{... | collective-permute-start | bytes 786440 | tf_op jit(solution)/shard_map/ppermute | solution.py:426
  26.5 0.7 %copy-start.3 = (f32[4,4,16,256]{3,2,1,0:T(8,128)}, f32[4,4,16,256]{3,2,1,0:T(8,128)S(1)}, u32[]{:S(2)}) copy-start(f32[4,4,16,256]{3,2,1,0:T(8,128)S(1)} %collective-permute-done.3.refs_4_) | copy-start | bytes 786436
  27.3 0.7 %copy-start.4 = (f32[4,4,16,256]{3,2,1,0:T(8,128)}, f32[4,4,16,256]{3,2,1,0:T(8,128)S(1)}, u32[]{:S(2)}) copy-start(f32[4,4,16,256]{3,2,1,0:T(8,128)S(1)} %collective-permute-done.4.refs_5_) | copy-start | bytes 786436
  48.0 4.5 %collective-permute-start.5 = (f32[4,24,256]{2,1,0:T(8,128)}, f32[4,24,256]{2,1,0:T(8,128)S(1)}, u32[]{:S(2)}, u32[]{:S(2)}) collective-permute-start(f32[4,24,256]{2,1,0:T(8,128)} %get-tuple-element.23), channel_id=1, source_target_pairs={{0,4},{4,8},{8,12},{12,0},{1,5},{5,9},{9,13},{13,1},{2,6},{6,10},{... | collective-permute-start | bytes 294920 | tf_op jit(solution)/shard_map/ppermute | solution.py:430
  48.3 5.9 %collective-permute-start.6 = (f32[4,24,256]{2,1,0:T(8,128)}, f32[4,24,256]{2,1,0:T(8,128)S(1)}, u32[]{:S(2)}, u32[]{:S(2)}) collective-permute-start(f32[4,24,256]{2,1,0:T(8,128)} %get-tuple-element.24), channel_id=1, source_target_pairs={{0,8},{4,12},{8,0},{12,4},{1,9},{5,13},{9,1},{13,5},{2,10},{6,14},... | collective-permute-start | bytes 294920 | tf_op jit(solution)/shard_map/ppermute | solution.py:430
  49.6 5.0 %collective-permute-start.7 = (f32[4,24,256]{2,1,0:T(8,128)}, f32[4,24,256]{2,1,0:T(8,128)S(1)}, u32[]{:S(2)}, u32[]{:S(2)}) collective-permute-start(f32[4,24,256]{2,1,0:T(8,128)} %get-tuple-element.25), channel_id=1, source_target_pairs={{0,12},{4,0},{8,4},{12,8},{1,13},{5,1},{9,5},{13,9},{2,14},{6,2},{... | collective-permute-start | bytes 294920 | tf_op jit(solution)/shard_map/ppermute | solution.py:430
where the time goes:
time: 56.9 us; the launch traced here: 56.1 us
  Pallas kernels  35.3 us (62%)
  starting transfers between devices  11.2 us (20%)
  waiting for transfers between devices  4.24 us (7%)
  local copies, waits for them, and re-layouts  3.02 us (5%)
  other arithmetic  1.6 us (3%)
  between operations  0.71 us (1%)
    pallas_call x1, Pallas kernels, depth_steps(): pl.pallas_call(functools.partial(depth_kernel, sizes), out_shape=(jax.Sha...  20 us
    pallas_call x2, Pallas kernels, inject(): pl.pallas_call(functools.partial(inject_kernel, rows, halo, row_count), o...  15.3 us
    ppermute x1, starting transfers between devices, body(): before = lax.ppermute(lowest, 'tile', up)  3.65 us
    ppermute x3, waiting for transfers between devices, body(): total = total + lax.ppermute(image, 'freq', pairs)  3.57 us
    ppermute x3, starting transfers between devices, body(): others = [lax.ppermute(velocity, 'freq', pairs) for pairs in shifts('freq')]  3.25 us
    ppermute x3, starting transfers between devices, body(): total = total + lax.ppermute(image, 'freq', pairs)  2.97 us
    unnamed x10, local copies, waits for them, and re-layouts  2.07 us
    add x1, other arithmetic, body(): total = total + lax.ppermute(image, 'freq', pairs)  1.56 us
  transfers between devices with their start and end apart: 8, of which 4 were waited for; matrix products, arithmetic and copies ran while one was open for 2% of the time, Pallas kernels for 27%

commit v1 on v0

--- a/solution.py
+++ b/solution.py
@@ -98,7 +98,7 @@
     whole = pl.BlockSpec(memory_space=pltpu.VMEM)
     return pl.pallas_call(
         functools.partial(inject_kernel, rows, halo, row_count),
-        out_shape=jax.ShapeDtypeStruct((2, cols // LANES, rows, LANES), jnp.float32),
+        out_shape=pltpu.VMEM((2, cols // LANES, rows, LANES), jnp.float32),
         in_specs=[whole, whole],
         out_specs=whole,
         cost_estimate=pl.CostEstimate(
@@ -168,8 +168,7 @@
     freqs = lax.axis_size("freq")
     tiles = lax.axis_size("tile")
     pieces, (before_ref, after_ref, src_ref, rec_ref) = refs[:freqs], refs[freqs : freqs + 4]
-    fields_ref, *image_refs = refs[freqs + 4 : 2 * freqs + 5]
-    terms, sums, speed, flat, sem = refs[2 * freqs + 5 :]
+    fields_ref, *image_refs, terms, sums, speed, flat, sem = refs[freqs + 4 :]
     me = lax.axis_index("freq")
     tile = lax.axis_index("tile")
     number = (me + 1).astype(jnp.float32)
@@ -192,10 +191,6 @@
             pending.pop(0).wait()
 
     copy.started = 0
-    for field, ref in enumerate((src_ref, rec_ref)):
-        for part in range(2):
-            copy(ref.at[part], terms.at[0, 2 * field + part, :, :rows, :])
-    arrived = pending[:]
     for back, piece in enumerate(pieces):
         owner = lax.rem(me + freqs - back, freqs)
         for part in range(per_owner):
@@ -239,11 +234,7 @@
         count = -(-(high - low) // SUB)
         return count + (count % SUB == 0)
 
-    for one in arrived:
-        one.wait()
-        pending.remove(one)
-
-    def one_pass(order, low, high):
+    def one_pass(plane, order, low, high):
         count = share(low, high)
         keeps = {}
         for row, keep in edges:
@@ -251,52 +242,57 @@
             if 0 <= at < SUB:
                 keeps.setdefault(index, []).append(jnp.where(sub == at, keep, 1.0))
 
-        def plane_body(plane, carry):
-            def load(part, index):
-                return terms[order - 1, plane, part, strided(low, count, index), :]
-
-            here = [load(part, 0) for part in range(parts)]
-            pair = [load(part, -1) + here[part] for part in range(parts)]
-            for index in range(count):
-                below = [load(part, index + 1) for part in range(parts)]
-                next_pair = [here[part] + below[part] for part in range(parts)]
-                stacked = [pair[part] + next_pair[part] for part in range(parts)]
-                moved = [pltpu.roll(v, LANES - 1 if part < blocks else 1, 1) for part, v in enumerate(stacked)]
-                for part in range(parts):
-                    blk = part % blocks
-                    even, odd = stacked[blk], stacked[blocks + blk]
-                    if part < blocks:
-                        other = moved[part + blocks - 1] if blk > 0 else zero
-                        side = jnp.where(first_lane, other, moved[part + blocks])
-                        total = (even + odd) + even + side
-                    else:
-                        other = moved[blk + 1] if blk + 1 < blocks else zero
-                        side = jnp.where(last_lane, other, moved[blk])
-                        total = (even + odd) + odd + side
-                    at = strided(low, count, index)
-                    if order == 1:
-                        total = 0.125 * total
-                    else:
-                        total = 0.25 * total - sums[plane, part, at, :]
-                    new = total - here[part]
-                    for keep in keeps.get(index, []):
-                        new = new * keep
-                        total = total * keep
-                    if order < PASSES:
-                        sums[plane, part, at, :] = total
-                    terms[order, plane, part, at, :] = new
-                here, pair = below, next_pair
-            return carry
-
-        lax.fori_loop(0, 4, plane_body, 0)
+        def load(part, index):
+            return terms[order - 1, plane, part, strided(low, count, index), :]
+
+        here = [load(part, 0) for part in range(parts)]
+        pair = [load(part, -1) + here[part] for part in range(parts)]
+        for index in range(count):
+            below = [load(part, index + 1) for part in range(parts)]
+            next_pair = [here[part] + below[part] for part in range(parts)]
+            stacked = [pair[part] + next_pair[part] for part in range(parts)]
+            moved = [pltpu.roll(v, LANES - 1 if part < blocks else 1, 1) for part, v in enumerate(stacked)]
+            for part in range(parts):
+                blk = part % blocks
+                even, odd = stacked[blk], stacked[blocks + blk]
+                if part < blocks:
+                    other = moved[part + blocks - 1] if blk > 0 else zero
+                    side = jnp.where(first_lane, other, moved[part + blocks])
+                    total = (even + odd) + even + side
+                else:
+                    other = moved[blk + 1] if blk + 1 < blocks else zero
+                    side = jnp.where(last_lane, other, moved[blk])
+                    total = (even + odd) + odd + side
+                at = strided(low, count, index)
+                if order == 1:
+                    total = 0.125 * total
+                else:
+                    total = 0.25 * total - sums[plane, part, at, :]
+                new = total - here[part]
+                for keep in keeps.get(index, []):
+                    new = new * keep
+                    total = total * keep
+                if order < PASSES:
+                    sums[plane, part, at, :] = total
+                terms[order, plane, part, at, :] = new
+            here, pair = below, next_pair
+
+    for field, ref in enumerate((src_ref, rec_ref)):
+        for part in range(2):
+            terms[0, 2 * field + part, :, :rows, :] = ref[part]
 
     def put(slot, blk, at, pair):
         for half, value in enumerate(join(*pair)):
             flat[slot, 2 * blk + half, at, :] = value
 
     for step in range(steps):
-        for order in range(1, PASSES + 1):
-            one_pass(order, PASSES * step + order, rows - PASSES * step - order)
+
+        def passes(plane, carry):
+            for order in range(1, PASSES + 1):
+                one_pass(plane, order, PASSES * step + order, rows - PASSES * step - order)
+            return carry
+
+        lax.fori_loop(0, 4, passes, 0)
         low, high = PASSES * (step + 1), rows - PASSES * (step + 1)
         count = share(low, high)
         last = step == steps - 1
@@ -355,16 +351,18 @@
 
             lax.fori_loop(0, image_count, correlate, 0)
 
-        for ahead, ref in enumerate(image_refs):
-            owner = lax.rem(me + ahead, freqs)
-            for part in range(per_owner):
-                lanes = slice(part * LANES, (part + 1) * LANES)
-                copy(flat.at[4 + step, owner * per_owner + part], ref.at[step, :, lanes])
+        for other, ref in enumerate(image_refs):
+            cores, places = len(image_refs), ref.shape[0]
+            core, place = lax.rem(me, cores), lax.div(me, cores)
+            for ahead in range(places):
+                owner = lax.rem(place + ahead, places) * cores + lax.rem(core + other, cores)
+                for part in range(per_owner):
+                    lanes = slice(part * LANES, (part + 1) * LANES)
+                    ref[ahead, step, :, lanes] = flat[4 + step, owner * per_owner + part]
     for plane in range(4):
         for part in range(parts):
             lanes = slice(part * LANES, (part + 1) * LANES)
-            copy(flat.at[plane, part], fields_ref.at[plane // 2, 0, plane % 2, :, lanes])
-    finish()
+            fields_ref[plane // 2, 0, plane % 2, :, lanes] = flat[plane, part]
 
 
 def depth_steps(pieces, before, after, src, rec, sizes):
@@ -374,27 +372,32 @@
     rows = row_count + 2 * halo
     parts = owners * width // LANES
     tall = row_count + 2 * vel_halo
-    there = pl.BlockSpec(memory_space=pltpu.HBM)
+    whole = pl.BlockSpec(memory_space=pltpu.VMEM)
+    cores = cores_of(owners)
     return pl.pallas_call(
         functools.partial(depth_kernel, sizes),
         out_shape=(
-            jax.ShapeDtypeStruct((2, 1, 2, row_count, owners * width), jnp.float32),
-            *[jax.ShapeDtypeStruct((steps, row_count, width), jnp.float32)] * owners,
+            pltpu.VMEM((2, 1, 2, row_count, owners * width), jnp.float32),
+            *[pltpu.VMEM((owners // cores, steps, row_count, width), jnp.float32)] * cores,
         ),
-        in_specs=[there] * (owners + 4),
-        out_specs=(there,) * (owners + 1),
+        in_specs=[whole] * (owners + 4),
+        out_specs=(whole,) * (cores + 1),
         scratch_shapes=[
             pltpu.VMEM((PASSES + 1, 4, parts, rows + 2 * SUB, LANES), jnp.float32),
             pltpu.VMEM((4, parts, rows + 2 * SUB, LANES), jnp.float32),
             pltpu.VMEM((steps, parts, tall + 2 * SUB, LANES), jnp.float32),
             pltpu.VMEM((4 + steps, parts, row_count, LANES), jnp.float32),
-            pltpu.SemaphoreType.DMA((4 + 3 * parts + (4 + steps) * parts,)),
+            pltpu.SemaphoreType.DMA((3 * parts,)),
         ],
         cost_estimate=pl.CostEstimate(
             flops=steps * 300 * rows * owners * width, bytes_accessed=64 * rows * owners * width, transcendentals=0
         ),
         name="depth",
-    )(*pieces, before, after, src, rec)
+    )(*[pltpu.with_memory_space_constraint(one, pltpu.VMEM) for one in (*pieces, before, after, src, rec)])
+
+
+def cores_of(freqs):
+    return 2 - freqs % 2
 
 
 def shifts(axis):
@@ -425,9 +428,16 @@
     before = lax.ppermute(lowest, "tile", up)
     after = lax.ppermute(highest, "tile", down)
     rec = inject(rec_cell, rec_data, rows, halo, row_count, cols)
-    fields, total, *images = depth_steps(pieces, before, after, src, rec, sizes)
-    for image, pairs in zip(images, shifts("freq")):
-        total = total + lax.ppermute(image, "freq", pairs)
+    fields, *images = depth_steps(pieces, before, after, src, rec, sizes)
+    cores = cores_of(freqs)
+    sums = images[0]
+    for other in range(1, cores):
+        swap = [(i, i - i % cores + (i + other) % cores) for i in range(freqs)]
+        sums = sums + lax.ppermute(images[other], "freq", swap)
+    total = sums[0]
+    for ahead in range(1, freqs // cores):
+        along = [(i, (i + ahead * cores) % freqs) for i in range(freqs)]
+        total = total + lax.ppermute(sums[ahead], "freq", along)
     return fields, total
 
 

time: 56.9 us -> 50.7 us (0.89)
  Pallas kernels: 35.3 us -> 31.9 us
  starting transfers between devices: 11.2 us -> 9.82 us
  local copies, waits for them, and re-layouts: 3.02 us -> 1.71 us
  waiting for transfers between devices: 4.24 us -> 5.51 us
  other arithmetic: 1.6 us -> 0.72 us
    pallas_call x1, Pallas kernels: 20 us -> 18.1 us  [depth_steps(): pl.pallas_call(functools.partial(depth_kernel, sizes), out_shape=(pltpu.V...]
    pallas_call x2, Pallas kernels: 15.3 us -> 13.8 us  [inject(): pl.pallas_call(functools.partial(inject_kernel, rows, halo, row_count), o...]
    ppermute x3 -> x2, starting transfers between devices: 2.97 us -> 1.6 us  [the longest x1 1.53 us: body(): total = total + lax.ppermute(sums[ahead], 'freq', along)]
    unnamed x10 -> x3, local copies, waits for them, and re-layouts: 2.07 us -> 0.75 us
    add x1 -> x2, other arithmetic: 1.56 us -> 0.68 us  [the longest x1 0.65 us: body(): total = total + lax.ppermute(sums[ahead], 'freq', along)]
    ppermute x3, waiting for transfers between devices: 0.67 us -> 1.45 us  [body(): others = [lax.ppermute(velocity, 'freq', pairs) for pairs in shifts('freq')]]
    ppermute x3 -> x2, waiting for transfers between devices: 3.57 us -> 4.06 us  [the longest x1 2.63 us: body(): total = total + lax.ppermute(sums[ahead], 'freq', along)]
  transfers between devices with their start and end apart: 8 -> 7, of which waited for: 4 -> 3; matrix products, arithmetic and copies ran while one was open for 2% -> 3% of each run, Pallas kernels for 27% -> 27%
where the time goes in v1:
time: 50.7 us; the launch traced here: 50.4 us
  Pallas kernels  31.9 us (63%)
  starting transfers between devices  9.82 us (19%)
  waiting for transfers between devices  5.51 us (11%)
  local copies, waits for them, and re-layouts  1.71 us (3%)
  between operations  0.76 us (1%)
  other arithmetic  0.72 us (1%)
    pallas_call x1, Pallas kernels, depth_steps(): pl.pallas_call(functools.partial(depth_kernel, sizes), out_shape=(pltpu.V...  18.1 us
    pallas_call x2, Pallas kernels, inject(): pl.pallas_call(functools.partial(inject_kernel, rows, halo, row_count), o...  13.8 us
    ppermute x1, starting transfers between devices, body(): before = lax.ppermute(lowest, 'tile', up)  3.68 us
    ppermute x3, starting transfers between devices, body(): others = [lax.ppermute(velocity, 'freq', pairs) for pairs in shifts('freq')]  3.25 us
    ppermute x1, waiting for transfers between devices, body(): total = total + lax.ppermute(sums[ahead], 'freq', along)  2.63 us
    ppermute x1, starting transfers between devices, body(): total = total + lax.ppermute(sums[ahead], 'freq', along)  1.53 us
    ppermute x3, waiting for transfers between devices, body(): others = [lax.ppermute(velocity, 'freq', pairs) for pairs in shifts('freq')]  1.45 us
    ppermute x1, waiting for transfers between devices, body(): sums = sums + lax.ppermute(images[other], 'freq', swap)  1.43 us
  transfers between devices with their start and end apart: 7, of which 3 were waited for; matrix products, arithmetic and copies ran while one was open for 3% of the time, Pallas kernels for 27%

profile of v1, /device:TPU:0, one launch (start us, length us, event | category | flops | bytes accessed | tf_op | source)
XLA Modules:
  0.0 50.4 jit_solution(14482923796802098586)
XLA Ops:
  0.6 2.5 %collective-permute-start.2 = (f32[4,24,256]{2,1,0:T(8,128)}, f32[4,24,256]{2,1,0:T(8,128)S(1)}, u32[]{:S(2)}, u32[]{:S(2)}) collective-permute-start(f32[4,24,256]{2,1,0:T(8,128)} %refs_0_.1), channel_id=1, source_target_pairs={{0,12},{4,0},{8,4},{12,8},{1,13},{5,1},{9,5},{13,9},{2,14},{6,2},{... | collective-permute-start | bytes 294920 | tf_op jit(solution)/shard_map/ppermute | solution.py:419
  3.1 0.6 %collective-permute-start.1 = (f32[4,24,256]{2,1,0:T(8,128)}, f32[4,24,256]{2,1,0:T(8,128)S(1)}, u32[]{:S(2)}, u32[]{:S(2)}) collective-permute-start(f32[4,24,256]{2,1,0:T(8,128)} %refs_0_.1), channel_id=1, source_target_pairs={{0,8},{4,12},{8,0},{12,4},{1,9},{5,13},{9,1},{13,5},{2,10},{6,14},... | collective-permute-start | bytes 294920 | tf_op jit(solution)/shard_map/ppermute | solution.py:419
  3.7 0.1 collective-permute-start
  3.9 0.9 %slice_bitcast_fusion.5 = (f32[1,4,16,256]{3,2,1,0:T(8,128)S(1)}, f32[1,4,16,256]{3,2,1,0:T(8,128)S(1)}) fusion(f32[4,24,256]{2,1,0:T(8,128)} %refs_0_.1), kind=kLoop, calls=%fused_computation.8 | loop fusion | bytes 262144 | tf_op jit(solution)/shard_map/stack | solution.py:426
  4.8 3.2 %inject.2.refs_6_ = f32[2,8,64,128]{3,2,1,0:T(8,128)S(1)} custom-call(s32[32,128]{1,0:T(8,128)} %bitcast.29, f32[2,32,128]{2,1,0:T(8,128)} %bitcast.28), custom_call_target="tpu_custom_call" | custom-call | flops 2147483648 | bytes 49152 | tf_op jit(solution)/shard_map/inject/pallas_call | solution.py:99
  8.0 0.0 collective-permute-done.2.refs_3_
  8.0 1.4 %collective-permute-done.1.refs_2_ = f32[4,24,256]{2,1,0:T(8,128)S(1)} collective-permute-done((f32[4,24,256]{2,1,0:T(8,128)}, f32[4,24,256]{2,1,0:T(8,128)S(1)}, u32[]{:S(2)}, u32[]{:S(2)}) %collective-permute-start.1) | collective-permute-done | bytes 98336 | tf_op jit(solution)/shard_map/ppermute | solution.py:419
  9.4 0.0 collective-permute-done.refs_1_
  9.5 3.7 %collective-permute-start.3 = (f32[4,4,16,256]{3,2,1,0:T(8,128)S(1)}, f32[4,4,16,256]{3,2,1,0:T(8,128)S(1)}, u32[]{:S(2)}, u32[]{:S(2)}) collective-permute-start(f32[4,4,16,256]{3,2,1,0:T(8,128)S(1)} %pad_maximum_fusion), channel_id=1, source_target_pairs={{0,1},{1,2},{2,3},{4,5},{5,6},{6,7},{8,9},{9,10},{10,11},{12,13},{... | collective-permute-start | bytes 786440 | tf_op jit(solution)/shard_map/ppermute | solution.py:428
  13.2 1.3 %collective-permute-start.4 = (f32[4,4,16,256]{3,2,1,0:T(8,128)S(1)}, f32[4,4,16,256]{3,2,1,0:T(8,128)S(1)}, u32[]{:S(2)}, u32[]{:S(2)}) collective-permute-start(f32[4,4,16,256]{3,2,1,0:T(8,128)S(1)} %pad_maximum_fusion.1), channel_id=1, source_target_pairs={{1,0},{2,1},{3,2},{5,4},{6,5},{7,6},{9,8},{10,9},{11,10},{13,12},{... | collective-permute-start | bytes 786440 | tf_op jit(solution)/shard_map/ppermute | solution.py:429
  14.5 0.0 copy-start
  14.5 10.6 %inject.3.refs_7_ = f32[2,8,64,128]{3,2,1,0:T(8,128)S(1)} custom-call(s32[128,128]{1,0:T(8,128)} %bitcast.27, f32[2,128,128]{2,1,0:T(8,128)} %bitcast.26), custom_call_target="tpu_custom_call" | custom-call | flops 8589934592 | bytes 196608 | tf_op jit(solution)/shard_map/inject/pallas_call | solution.py:99
  25.1 0.0 collective-permute-done.3.refs_4_
  25.2 0.0 collective-permute-done.4.refs_5_
  25.2 0.0 copy-done
  25.2 18.1 %depth.1 = (f32[2,1,2,24,1024]{4,3,2,1,0:T(8,128)S(1)}, f32[2,4,24,256]{3,2,1,0:T(8,128)S(1)}, f32[2,4,24,256]{3,2,1,0:T(8,128)S(1)}) custom-call(f32[4,24,256]{2,1,0:T(8,128)S(1)} %copy-done, f32[4,24,256]{2,1,0:T(8,128)S(1)} %collective-permute-done.refs_1_, f32[4,24,256]{2,1,0:T(8,128)S(1)} %collective-permute-done.1.refs_2_, ...), custom_call_target="tpu_custom_call" | custom-call | flops 78643200 | bytes 4194304 | tf_op jit(solution)/shard_map/depth/pallas_call | solution.py:377
  43.3 0.1 collective-permute-start.5
  43.4 1.4 %collective-permute-done.5 = f32[2,4,24,256]{3,2,1,0:T(8,128)S(1)} collective-permute-done((f32[2,4,24,256]{3,2,1,0:T(8,128)S(1)}, f32[2,4,24,256]{3,2,1,0:T(8,128)S(1)}, u32[]{:S(2)}, u32[]{:S(2)}) %collective-permute-start.5) | collective-permute-done | bytes 196640 | tf_op jit(solution)/shard_map/ppermute | solution.py:436
  44.9 1.5 %collective-permute-start.6 = (f32[4,24,256]{2,1,0:T(8,128)S(1)}, f32[4,24,256]{2,1,0:T(8,128)S(1)}, u32[]{:S(2)}, u32[]{:S(2)}) collective-permute-start(f32[4,24,256]{2,1,0:T(8,128)S(1)} %slice_bitcast_fusion), channel_id=1, source_target_pairs={{0,8},{4,12},{8,0},{12,4},{1,9},{5,13},{9,1},{13,5},{2,10},{6,14},... | collective-permute-start | bytes 294920 | tf_op jit(solution)/shard_map/ppermute | solution.py:440
  46.4 0.7 %copy.7 = f32[2,1,2,24,1024]{4,3,2,1,0:T(8,128)} copy(f32[2,1,2,24,1024]{4,3,2,1,0:T(8,128)S(1)} %get-tuple-element.32) | data formatting | bytes 786432
  47.2 2.6 %collective-permute-done.6 = f32[4,24,256]{2,1,0:T(8,128)S(1)} collective-permute-done((f32[4,24,256]{2,1,0:T(8,128)S(1)}, f32[4,24,256]{2,1,0:T(8,128)S(1)}, u32[]{:S(2)}, u32[]{:S(2)}) %collective-permute-start.6) | collective-permute-done | bytes 98336 | tf_op jit(solution)/shard_map/ppermute | solution.py:440
  49.8 0.7 %fusion = f32[4,24,256]{2,1,0:T(8,128)} fusion(f32[4,24,256]{2,1,0:T(8,128)S(1)} %collective-permute-done.6, f32[2,4,24,256]{3,2,1,0:T(8,128)S(1)} %add.6), kind=kLoop, calls=%fused_computation.4 | loop fusion | flops 24576 | bytes 294912 | tf_op jit(solution)/shard_map/add | solution.py:440
  (6 shorter events, 0.1 us)
Async XLA Ops:
  0.6 7.3 %collective-permute-start.2 = (f32[4,24,256]{2,1,0:T(8,128)}, f32[4,24,256]{2,1,0:T(8,128)S(1)}, u32[]{:S(2)}, u32[]{:S(2)}) collective-permute-start(f32[4,24,256]{2,1,0:T(8,128)} %refs_0_.1), channel_id=1, source_target_pairs={{0,12},{4,0},{8,4},{12,8},{1,13},{5,1},{9,5},{13,9},{2,14},{6,2},{... | collective-permute-start | bytes 294920 | tf_op jit(solution)/shard_map/ppermute | solution.py:419
  3.1 6.3 %collective-permute-start.1 = (f32[4,24,256]{2,1,0:T(8,128)}, f32[4,24,256]{2,1,0:T(8,128)S(1)}, u32[]{:S(2)}, u32[]{:S(2)}) collective-permute-start(f32[4,24,256]{2,1,0:T(8,128)} %refs_0_.1), channel_id=1, source_target_pairs={{0,8},{4,12},{8,0},{12,4},{1,9},{5,13},{9,1},{13,5},{2,10},{6,14},... | collective-permute-start | bytes 294920 | tf_op jit(solution)/shard_map/ppermute | solution.py:419
  3.7 5.7 %collective-permute-start = (f32[4,24,256]{2,1,0:T(8,128)}, f32[4,24,256]{2,1,0:T(8,128)S(1)}, u32[]{:S(2)}, u32[]{:S(2)}) collective-permute-start(f32[4,24,256]{2,1,0:T(8,128)} %refs_0_.1), channel_id=1, source_target_pairs={{0,4},{4,8},{8,12},{12,0},{1,5},{5,9},{9,13},{13,1},{2,6},{6,10},{... | collective-permute-start | bytes 294920 | tf_op jit(solution)/shard_map/ppermute | solution.py:419
  9.5 15.6 %collective-permute-start.3 = (f32[4,4,16,256]{3,2,1,0:T(8,128)S(1)}, f32[4,4,16,256]{3,2,1,0:T(8,128)S(1)}, u32[]{:S(2)}, u32[]{:S(2)}) collective-permute-start(f32[4,4,16,256]{3,2,1,0:T(8,128)S(1)} %pad_maximum_fusion), channel_id=1, source_target_pairs={{0,1},{1,2},{2,3},{4,5},{5,6},{6,7},{8,9},{9,10},{10,11},{12,13},{... | collective-permute-start | bytes 786440 | tf_op jit(solution)/shard_map/ppermute | solution.py:428
  13.2 11.9 %collective-permute-start.4 = (f32[4,4,16,256]{3,2,1,0:T(8,128)S(1)}, f32[4,4,16,256]{3,2,1,0:T(8,128)S(1)}, u32[]{:S(2)}, u32[]{:S(2)}) collective-permute-start(f32[4,4,16,256]{3,2,1,0:T(8,128)S(1)} %pad_maximum_fusion.1), channel_id=1, source_target_pairs={{1,0},{2,1},{3,2},{5,4},{6,5},{7,6},{9,8},{10,9},{11,10},{13,12},{... | collective-permute-start | bytes 786440 | tf_op jit(solution)/shard_map/ppermute | solution.py:429
  14.5 10.6 %copy-start = (f32[4,24,256]{2,1,0:T(8,128)S(1)}, f32[4,24,256]{2,1,0:T(8,128)}, u32[]{:S(2)}) copy-start(f32[4,24,256]{2,1,0:T(8,128)} %refs_0_.1) | copy-start | bytes 294916
  43.3 1.5 %collective-permute-start.5 = (f32[2,4,24,256]{3,2,1,0:T(8,128)S(1)}, f32[2,4,24,256]{3,2,1,0:T(8,128)S(1)}, u32[]{:S(2)}, u32[]{:S(2)}) collective-permute-start(f32[2,4,24,256]{3,2,1,0:T(8,128)S(1)} %get-tuple-element.21), channel_id=1, source_target_pairs={{0,4},{4,0},{8,12},{12,8},{1,5},{5,1},{9,13},{13,9},{2,6},{6,2},{1... | collective-permute-start | bytes 589832 | tf_op jit(solution)/shard_map/ppermute | solution.py:436
  44.9 4.9 %collective-permute-start.6 = (f32[4,24,256]{2,1,0:T(8,128)S(1)}, f32[4,24,256]{2,1,0:T(8,128)S(1)}, u32[]{:S(2)}, u32[]{:S(2)}) collective-permute-start(f32[4,24,256]{2,1,0:T(8,128)S(1)} %slice_bitcast_fusion), channel_id=1, source_target_pairs={{0,8},{4,12},{8,0},{12,4},{1,9},{5,13},{9,1},{13,5},{2,10},{6,14},... | collective-permute-start | bytes 294920 | tf_op jit(solution)/shard_map/ppermute | solution.py:440
